TPU v7x, 32 devices: a whole 2x2x4 slice. The times are simulated.
32 devices in a mesh: dp: 16 (over z, x, core), seq: 2 (over y).
Axes of the slice: x: 2, y: 2, z: 4, core: 2. Of those that a mesh axis runs over, the one named last changes fastest.
Arguments:
- images: bfloat16 [32, 592, 1024], P('dp', 'seq'), may hold values from -6 to 6
- cotangent: bfloat16 [32, 592, 1024], P('dp', 'seq'), may hold values from -6 to 6
- w_qkv: float32 [1024, 3072], P('dp', 'seq'), may hold values from -0.1875 to 0.1875
- w_out: float32 [1024, 1024], P('dp', 'seq'), may hold values from -1 to 1
- w_up: float32 [1024, 4096], P('dp', 'seq'), may hold values from -0.1875 to 0.1875
- w_down: float32 [4096, 1024], P('dp', 'seq'), may hold values from -0.09375 to 0.09375
- gains: float32 [2, 1024], P(None, ('dp', 'seq')), may hold values from 0.5 to 1.5
- biases: float32 [10, 1024], P(None, ('dp', 'seq')), may hold values from -3 to 3
- first_qkv: float32 [1024, 3072], P('dp', 'seq'), may hold values from -120 to 120
- first_out: float32 [1024, 1024], P('dp', 'seq'), may hold values from -120 to 120
- first_up: float32 [1024, 4096], P('dp', 'seq'), may hold values from -120 to 120
- first_down: float32 [4096, 1024], P('dp', 'seq'), may hold values from -120 to 120
- first_gains: float32 [2, 1024], P(None, ('dp', 'seq')), may hold values from -120 to 120
- first_biases: float32 [10, 1024], P(None, ('dp', 'seq')), may hold values from -120 to 120
- second_qkv: float32 [1024, 3072], P('dp', 'seq'), may hold values from 100 to 10000
- second_out: float32 [1024, 1024], P('dp', 'seq'), may hold values from 100 to 10000
- second_up: float32 [1024, 4096], P('dp', 'seq'), may hold values from 100 to 10000
- second_down: float32 [4096, 1024], P('dp', 'seq'), may hold values from 100 to 10000
- second_gains: float32 [2, 1024], P(None, ('dp', 'seq')), may hold values from 100 to 10000
- second_biases: float32 [10, 1024], P(None, ('dp', 'seq')), may hold values from 100 to 10000
Outputs:
- out_images: bfloat16 [32, 592, 1024], P('dp', 'seq')
- grad_images: bfloat16 [32, 592, 1024], P('dp', 'seq')
- grad_qkv: float32 [1024, 3072], P('dp', 'seq')
- grad_out: float32 [1024, 1024], P('dp', 'seq')
- grad_up: float32 [1024, 4096], P('dp', 'seq')
- grad_down: float32 [4096, 1024], P('dp', 'seq')
- grad_gains: float32 [2, 1024], P(None, ('dp', 'seq'))
- grad_biases: float32 [10, 1024], P(None, ('dp', 'seq'))
- new_qkv: float32 [1024, 3072], P('dp', 'seq')
- new_out: float32 [1024, 1024], P('dp', 'seq')
- new_up: float32 [1024, 4096], P('dp', 'seq')
- new_down: float32 [4096, 1024], P('dp', 'seq')
- new_gains: float32 [2, 1024], P(None, ('dp', 'seq'))
- new_biases: float32 [10, 1024], P(None, ('dp', 'seq'))
- new_first_qkv: float32 [1024, 3072], P('dp', 'seq')
- new_first_out: float32 [1024, 1024], P('dp', 'seq')
- new_first_up: float32 [1024, 4096], P('dp', 'seq')
- new_first_down: float32 [4096, 1024], P('dp', 'seq')
- new_first_gains: float32 [2, 1024], P(None, ('dp', 'seq'))
- new_first_biases: float32 [10, 1024], P(None, ('dp', 'seq'))
- new_second_qkv: float32 [1024, 3072], P('dp', 'seq')
- new_second_out: float32 [1024, 1024], P('dp', 'seq')
- new_second_up: float32 [1024, 4096], P('dp', 'seq')
- new_second_down: float32 [4096, 1024], P('dp', 'seq')
- new_second_gains: float32 [2, 1024], P(None, ('dp', 'seq'))
- new_second_biases: float32 [10, 1024], P(None, ('dp', 'seq'))
All inputs are finite; a program needn't handle non-finite values.
Results may differ from a plain program's by a relative error of at most 0.028.
Values may be sent and summed in bfloat16 or wider, within the bound.
A program may use at most 256 MiB of HBM per device.

v0:
```python
import jax
import jax.numpy as jnp
from jax import lax
from jax.sharding import PartitionSpec as P

HEAD_DIM = 64
PATCH_TOK = 577
STEP = 5


def normalize(rows):
    center = rows - jnp.mean(rows, axis=-1, keepdims=True)
    inverse = lax.rsqrt(jnp.mean(center * center, axis=-1, keepdims=True) + 1e-06)
    return (center * inverse, inverse)


def norm_back(grad_out, normed, inverse, gain):
    scaled = grad_out * gain
    return inverse * (
        scaled
        - jnp.mean(scaled, axis=-1, keepdims=True)
        - normed * jnp.mean(scaled * normed, axis=-1, keepdims=True)
    )


def gelu_value(pre):
    return pre * 0.5 * (1.0 + lax.erf(pre * 0.7071067811865476))


def gelu_slope(pre):
    return (
        0.5 * (1.0 + lax.erf(pre * 0.7071067811865476))
        + pre * jnp.exp(-0.5 * pre * pre) * 0.3989422804014327
    )


def adamw(param, grad, first, second):
    first_new = 0.9 * first + 0.1 * grad
    second_new = 0.95 * second + 0.05 * grad * grad
    step_size = first_new / (1.0 - 0.9**STEP) / (jnp.sqrt(second_new / (1.0 - 0.95**STEP)) + 1e-08)
    return (param - 0.004 * (step_size + 0.05 * param), first_new, second_new)


def body(
    images,
    cotangent,
    w_qkv,
    w_out,
    w_up,
    w_down,
    gains,
    biases,
    first_qkv,
    first_out,
    first_up,
    first_down,
    first_gains,
    first_biases,
    second_qkv,
    second_out,
    second_up,
    second_down,
    second_gains,
    second_biases,
):
    params = (w_qkv, w_out, w_up, w_down, gains, biases)
    firsts = (first_qkv, first_out, first_up, first_down, first_gains, first_biases)
    seconds = (second_qkv, second_out, second_up, second_down, second_gains, second_biases)
    kernels = tuple((param.astype(jnp.bfloat16) for param in params))
    block_parts = (
        lax.all_gather(kernels[0], "seq", axis=1, tiled=True),
        lax.all_gather(kernels[1], "seq", axis=1, tiled=True),
        lax.all_gather(kernels[2], "seq", axis=1, tiled=True),
        lax.all_gather(kernels[3], "seq", axis=1, tiled=True),
        lax.all_gather(kernels[4], "seq", axis=1, tiled=True),
        lax.all_gather(kernels[5], "seq", axis=1, tiled=True),
    )
    wide_qkv, wide_out, wide_up, wide_down, wide_gains, wide_biases = (
        lax.all_gather(block_parts[0], "dp", axis=0, tiled=True),
        lax.all_gather(block_parts[1], "dp", axis=0, tiled=True),
        lax.all_gather(block_parts[2], "dp", axis=0, tiled=True),
        lax.all_gather(block_parts[3], "dp", axis=0, tiled=True),
        lax.all_gather(block_parts[4], "dp", axis=1, tiled=True),
        lax.all_gather(block_parts[5], "dp", axis=1, tiled=True),
    )
    count, group, width = images.shape
    heads = width // HEAD_DIM
    scale = HEAD_DIM ** (-0.5)
    pad_len = group * lax.axis_size("seq")
    offset = lax.axis_index("seq") * group
    query_live = offset + jnp.arange(group, dtype=jnp.int32) < PATCH_TOK
    key_live = jnp.arange(pad_len, dtype=jnp.int32) < PATCH_TOK
    gain = wide_gains.astype(jnp.float32)
    bias = wide_biases.astype(jnp.float32)
    rows = images.astype(jnp.float32)
    normed_a, inverse_a = normalize(rows)
    hidden_a = (normed_a * gain[0] + bias[0]).astype(jnp.bfloat16)
    mixed = jnp.einsum("icd,de->ice", hidden_a, wide_qkv, preferred_element_type=jnp.float32)
    queries = (mixed[..., :width] + bias[1]).astype(jnp.bfloat16)
    keys = mixed[..., width : 2 * width].astype(jnp.bfloat16)
    values = (mixed[..., 2 * width :] + bias[2]).astype(jnp.bfloat16)
    keys_all, values_all = (
        lax.all_gather(keys, "seq", axis=1, tiled=True),
        lax.all_gather(values, "seq", axis=1, tiled=True),
    )
    query_heads = queries.reshape(count, group, heads, HEAD_DIM)
    key_heads = keys_all.reshape(count, pad_len, heads, HEAD_DIM)
    value_heads = values_all.reshape(count, pad_len, heads, HEAD_DIM)

    def score_block():
        scores = (
            jnp.einsum(
                "ichd,ishd->ihcs", query_heads, key_heads, preferred_element_type=jnp.float32
            )
            * scale
        )
        return jnp.where(key_live[None, None, None, :], scores, -1e30)

    scores = score_block()
    top = jnp.max(scores, axis=-1, keepdims=True)
    lse = top + jnp.log(jnp.sum(jnp.exp(scores - top), axis=-1, keepdims=True))
    probs_b = jnp.exp(scores - lse).astype(jnp.bfloat16)
    context = (
        jnp.einsum("ihcs,ishd->ichd", probs_b, value_heads, preferred_element_type=jnp.float32)
        .reshape(count, group, width)
        .astype(jnp.bfloat16)
    )
    resid = (
        rows
        + jnp.einsum("icd,de->ice", context, wide_out, preferred_element_type=jnp.float32)
        + bias[3]
    )
    normed_b, inverse_b = normalize(resid)
    hidden_b = (normed_b * gain[1] + bias[4]).astype(jnp.bfloat16)
    pre = jnp.einsum("icd,df->icf", hidden_b, wide_up, preferred_element_type=jnp.float32) + bias[
        6:
    ].reshape(-1)
    active = gelu_value(pre).astype(jnp.bfloat16)
    out_images = (
        resid
        + jnp.einsum("icf,fd->icd", active, wide_down, preferred_element_type=jnp.float32)
        + bias[5]
    ).astype(jnp.bfloat16)
    back_qkv, back_out, back_up, back_down, back_gains = (
        wide_qkv,
        wide_out,
        wide_up,
        wide_down,
        wide_gains,
    )
    back_gain = back_gains.astype(jnp.float32)
    grad_y = cotangent.astype(jnp.float32) * query_live[None, :, None].astype(jnp.float32)
    grad_yb = grad_y.astype(jnp.bfloat16)
    g_down = jnp.einsum("icf,icd->fd", active, grad_yb, preferred_element_type=jnp.float32)
    grad_pre = jnp.einsum(
        "icd,fd->icf", grad_yb, back_down, preferred_element_type=jnp.float32
    ) * gelu_slope(pre)
    grad_preb = grad_pre.astype(jnp.bfloat16)
    g_up = jnp.einsum("icd,icf->df", hidden_b, grad_preb, preferred_element_type=jnp.float32)
    grad_hb = jnp.einsum("icf,df->icd", grad_preb, back_up, preferred_element_type=jnp.float32)
    grad_resid = grad_y + norm_back(grad_hb, normed_b, inverse_b, back_gain[1])
    grad_rb = grad_resid.astype(jnp.bfloat16)
    g_outw = jnp.einsum("icd,ice->de", context, grad_rb, preferred_element_type=jnp.float32)
    grad_ctx = (
        jnp.einsum("ice,de->icd", grad_rb, back_out, preferred_element_type=jnp.float32)
        .astype(jnp.bfloat16)
        .reshape(count, group, heads, HEAD_DIM)
    )
    probs = jnp.exp(score_block() - lse)
    grad_probs = jnp.einsum(
        "ichd,ishd->ihcs", grad_ctx, value_heads, preferred_element_type=jnp.float32
    )
    part_v = jnp.einsum(
        "ihcs,ichd->ishd", probs.astype(jnp.bfloat16), grad_ctx, preferred_element_type=jnp.float32
    ).reshape(count, pad_len, width)
    delta = jnp.sum(probs * grad_probs, axis=-1, keepdims=True)
    grad_scores = (probs * (grad_probs - delta) * scale).astype(jnp.bfloat16)
    grad_q = jnp.einsum(
        "ihcs,ishd->ichd", grad_scores, key_heads, preferred_element_type=jnp.float32
    ).reshape(count, group, width)
    part_k = jnp.einsum(
        "ihcs,ichd->ishd", grad_scores, query_heads, preferred_element_type=jnp.float32
    ).reshape(count, pad_len, width)
    grad_k, grad_v = (
        lax.psum_scatter(
            part_k.astype(jnp.bfloat16), "seq", scatter_dimension=1, tiled=True
        ).astype(jnp.float32),
        lax.psum_scatter(
            part_v.astype(jnp.bfloat16), "seq", scatter_dimension=1, tiled=True
        ).astype(jnp.float32),
    )
    grad_mixed = jnp.concatenate([grad_q, grad_k, grad_v], axis=-1).astype(jnp.bfloat16)
    g_qkv = jnp.einsum("icd,ice->de", hidden_a, grad_mixed, preferred_element_type=jnp.float32)
    grad_ha = jnp.einsum("ice,de->icd", grad_mixed, back_qkv, preferred_element_type=jnp.float32)
    grad_images = (grad_resid + norm_back(grad_ha, normed_a, inverse_a, back_gain[0])).astype(
        jnp.bfloat16
    )
    g_gains = jnp.stack(
        [jnp.sum(grad_ha * normed_a, axis=(0, 1)), jnp.sum(grad_hb * normed_b, axis=(0, 1))]
    )
    g_biases = jnp.concatenate(
        [
            jnp.stack(
                [
                    jnp.sum(grad_ha, axis=(0, 1)),
                    jnp.sum(grad_q, axis=(0, 1)),
                    jnp.sum(grad_v, axis=(0, 1)),
                    jnp.sum(grad_resid, axis=(0, 1)),
                    jnp.sum(grad_hb, axis=(0, 1)),
                    jnp.sum(grad_y, axis=(0, 1)),
                ]
            ),
            jnp.sum(grad_pre, axis=(0, 1)).reshape(-1, width),
        ],
        axis=0,
    )
    partial_sums = (
        lax.psum_scatter(g_qkv.astype(jnp.bfloat16), "dp", scatter_dimension=0, tiled=True).astype(
            jnp.float32
        ),
        lax.psum_scatter(g_outw.astype(jnp.bfloat16), "dp", scatter_dimension=0, tiled=True).astype(
            jnp.float32
        ),
        lax.psum_scatter(g_up.astype(jnp.bfloat16), "dp", scatter_dimension=0, tiled=True).astype(
            jnp.float32
        ),
        lax.psum_scatter(g_down.astype(jnp.bfloat16), "dp", scatter_dimension=0, tiled=True).astype(
            jnp.float32
        ),
        lax.psum_scatter(
            g_gains.astype(jnp.bfloat16), "dp", scatter_dimension=1, tiled=True
        ).astype(jnp.float32),
        lax.psum_scatter(
            g_biases.astype(jnp.bfloat16), "dp", scatter_dimension=1, tiled=True
        ).astype(jnp.float32),
    )
    totals = (
        lax.psum_scatter(
            partial_sums[0].astype(jnp.bfloat16), "seq", scatter_dimension=1, tiled=True
        ).astype(jnp.float32),
        lax.psum_scatter(
            partial_sums[1].astype(jnp.bfloat16), "seq", scatter_dimension=1, tiled=True
        ).astype(jnp.float32),
        lax.psum_scatter(
            partial_sums[2].astype(jnp.bfloat16), "seq", scatter_dimension=1, tiled=True
        ).astype(jnp.float32),
        lax.psum_scatter(
            partial_sums[3].astype(jnp.bfloat16), "seq", scatter_dimension=1, tiled=True
        ).astype(jnp.float32),
        lax.psum_scatter(
            partial_sums[4].astype(jnp.bfloat16), "seq", scatter_dimension=1, tiled=True
        ).astype(jnp.float32),
        lax.psum_scatter(
            partial_sums[5].astype(jnp.bfloat16), "seq", scatter_dimension=1, tiled=True
        ).astype(jnp.float32),
    )
    updated = [
        adamw(param, grad, first, second)
        for param, grad, first, second in zip(params, totals, firsts, seconds)
    ]
    news = tuple((entry[0] for entry in updated))
    new_firsts = tuple((entry[1] for entry in updated))
    new_seconds = tuple((entry[2] for entry in updated))
    return (
        out_images,
        grad_images,
        totals[0],
        totals[1],
        totals[2],
        totals[3],
        totals[4],
        totals[5],
        news[0],
        news[1],
        news[2],
        news[3],
        news[4],
        news[5],
        new_firsts[0],
        new_firsts[1],
        new_firsts[2],
        new_firsts[3],
        new_firsts[4],
        new_firsts[5],
        new_seconds[0],
        new_seconds[1],
        new_seconds[2],
        new_seconds[3],
        new_seconds[4],
        new_seconds[5],
    )


def solution(mesh):
    return jax.shard_map(
        body,
        mesh=mesh,
        in_specs=(
            P("dp", "seq", None),
            P("dp", "seq", None),
            P("dp", "seq"),
            P("dp", "seq"),
            P("dp", "seq"),
            P("dp", "seq"),
            P(None, ("dp", "seq")),
            P(None, ("dp", "seq")),
            P("dp", "seq"),
            P("dp", "seq"),
            P("dp", "seq"),
            P("dp", "seq"),
            P(None, ("dp", "seq")),
            P(None, ("dp", "seq")),
            P("dp", "seq"),
            P("dp", "seq"),
            P("dp", "seq"),
            P("dp", "seq"),
            P(None, ("dp", "seq")),
            P(None, ("dp", "seq")),
        ),
        out_specs=(
            P("dp", "seq", None),
            P("dp", "seq", None),
            P("dp", "seq"),
            P("dp", "seq"),
            P("dp", "seq"),
            P("dp", "seq"),
            P(None, ("dp", "seq")),
            P(None, ("dp", "seq")),
            P("dp", "seq"),
            P("dp", "seq"),
            P("dp", "seq"),
            P("dp", "seq"),
            P(None, ("dp", "seq")),
            P(None, ("dp", "seq")),
            P("dp", "seq"),
            P("dp", "seq"),
            P("dp", "seq"),
            P("dp", "seq"),
            P(None, ("dp", "seq")),
            P(None, ("dp", "seq")),
            P("dp", "seq"),
            P("dp", "seq"),
            P("dp", "seq"),
            P("dp", "seq"),
            P(None, ("dp", "seq")),
            P(None, ("dp", "seq")),
        ),
        check_vma=False,
    )
```

profile of v0, /device:TPU:0, one launch (start us, length us, event | category | flops | bytes accessed | tf_op | source)
XLA Modules:
  0.0 1155.0 jit_solution(3185854335412844673)
XLA Ops:
  22.2 22.7 %all-gather.3 = bf16[16,64,10]{1,2,0:T(8,128)(2,1)S(1)} all-gather(bf16[1,64,10]{1,2,0:T(8,128)(2,1)S(1)} %reshape.162), channel_id=1, replica_groups=mesh['dp'=16,'seq'=2] {'dp'}, dimensions={0}, use_global_device_ids=true | all-gather | bytes 21760 | tf_op jit(solution)/shard_map/all_gather | solution.py:84
  50.0 17.9 %all-gather.1 = bf16[16,64,2]{1,2,0:T(2,128)(2,1)S(1)} all-gather(bf16[1,64,2]{1,2,0:T(2,128)(2,1)S(1)} %reshape.158), channel_id=1, replica_groups=mesh['dp'=16,'seq'=2] {'dp'}, dimensions={0}, use_global_device_ids=true | all-gather | bytes 4352 | tf_op jit(solution)/shard_map/all_gather | solution.py:83
  69.4 10.9 all-gather.11.cloned.1.call-done
  99.1 14.9 %all_gather.52 = bf16[64,4096]{1,0:T(8,128)(2,1)} all-gather(bf16[64,2048]{1,0:T(8,128)(2,1)S(1)} %convert_element_type.171), channel_id=1, replica_groups=mesh['dp'=16,'seq'=2] {'seq'}, dimensions={1}, use_global_device_ids=true | all-gather | bytes 786432 | tf_op jit(solution)/shard_map/all_gather | solution.py:73
  116.3 15.7 %all-gather.13.cloned.1.call-done = bf16[2,592,1024]{2,1,0:T(8,128)(2,1)} async-done(((bf16[2,296,1024]{2,1,0:T(8,128)(2,1)}), bf16[2,592,1024]{2,1,0:T(8,128)(2,1)}) %all-gather.13.cloned.1.call-update) | async-done | bytes 2424848 | tf_op jit(solution)/shard_map/all_gather | solution.py:104
  136.4 33.9 %all-gather.15.cloned.1.call-done = bf16[2,592,1024]{2,1,0:T(8,128)(2,1)} async-done(((bf16[2,296,1024]{2,1,0:T(8,128)(2,1)}), bf16[2,592,1024]{2,1,0:T(8,128)(2,1)}) %all-gather.15.cloned.1.call-update) | async-done | bytes 2424848 | tf_op jit(solution)/shard_map/all_gather | solution.py:103
  174.7 14.2 %fusion.2 = (f32[2,16,296]{2,1,0:T(8,128)S(1)}, f32[2,16,296,592]{3,2,1,0:T(8,128)}) fusion(pred[592]{0:T(1024)(128)(4,1)S(1)} %iota_compare_fusion, bf16[2,296,16,64]{1,3,2,0:T(8,128)(2,1)S(1)} %bitcast.138, bf16[2,592,16,64]{1,3,2,0:T(8,128)(2,1)} %bitcast.130), kind=kOutput, calls=%fused_computation.7 | convolution fusion | flops 734563072 | bytes 26105424 | tf_op jit(solution)/shard_map/ichd,ishd->ihcs/dot_general | solution.py:112
  188.9 9.5 exponential_reduce_fusion
  198.4 10.8 convolution_convert_fusion.1
  219.1 69.8 %all-gather.19.cloned.1.call-done = bf16[1024,4096]{1,0:T(8,128)(2,1)} async-done(((bf16[64,4096]{1,0:T(8,128)(2,1)}), bf16[1024,4096]{1,0:T(8,128)(2,1)}) %all-gather.19.cloned.1.call-update) | async-done | bytes 8388624 | tf_op jit(solution)/shard_map/all_gather | solution.py:81
  288.9 12.3 %multiply_convert_fusion.1 = (bf16[2,296,4096]{2,1,0:T(8,128)(2,1)S(1)}, f32[2,296,4096]{2,1,0:T(8,128)}) fusion(f32[4096]{0:T(1024)S(1)} %bitcast.159, bf16[1024,4096]{1,0:T(8,128)(2,1)} %all-gather.19.cloned.1.call-done, f32[2,296,1024]{2,1,0:T(8,128)} %copy-done.3, f32[1024]{0:T(1024)S(1)} %bitcast.166, f32[1024]{0:T(1024)S(1)} %bitcast.155, ...), kind=kOutput, calls=%fused_computation.21 | convolution fusion | flops 4983635968 | bytes 25391744 | tf_op jit(solution)/shard_map/icd,df->icf/dot_general | solution.py:135
  303.4 9.2 bitcast_convert_fusion
  312.7 102.2 %reduce-scatter.39.cloned.1.call-done = bf16[256,1024]{1,0:T(8,128)(2,1)} async-done(((bf16[4096,1024]{1,0:T(8,128)(2,1)}), bf16[256,1024]{1,0:T(8,128)(2,1)}) %reduce-scatter.39.cloned.1.call-update) | async-done | bytes 524304 | tf_op jit(solution)/shard_map/reduce_scatter | solution.py:227
  414.9 16.5 %reduce-scatter.41.cloned.1.call-done = bf16[256,512]{1,0:T(8,128)(2,1)} async-done(((bf16[256,1024]{1,0:T(8,128)(2,1)}), bf16[256,512]{1,0:T(8,128)(2,1)}) %reduce-scatter.41.cloned.1.call-update) | async-done | bytes 262160 | tf_op jit(solution)/shard_map/reduce_scatter | solution.py:247
  442.7 74.4 %all-gather.21.cloned.1.call-done = bf16[4096,1024]{1,0:T(8,128)(2,1)} async-done(((bf16[256,1024]{1,0:T(8,128)(2,1)}), bf16[4096,1024]{1,0:T(8,128)(2,1)}) %all-gather.21.cloned.1.call-update) | async-done | bytes 8388624 | tf_op jit(solution)/shard_map/all_gather | solution.py:82
  517.1 12.6 %fusion.112 = (bf16[4096]{0:T(1024)(128)(2,1)S(1)}, bf16[2,296,4096]{2,1,0:T(8,128)(2,1)S(1)}) fusion(f32[2,296,4096]{2,1,0:T(8,128)} %get-tuple-element.77, f32[4096]{0:T(1024)S(1)} %bitcast.160, bf16[4096,1024]{1,0:T(8,128)(2,1)} %all-gather.21.cloned.1.call-done, bf16[2,296,1024]{2,1,0:T(8,128)(2,1)S(1)} %copy-done.13, f32[296]{0:T(512)} %copy-done.32), kind=kOutput, calls=%fused_computation.148 | convolution fusion | flops 4996968448 | bytes 24175776 | tf_op jit(solution)/shard_map/icd,fd->icf/dot_general | solution.py:155
  529.7 10.3 multiply_reduce_fusion.1
  547.1 12.0 %convolution_convert_fusion = bf16[2,16,64,592]{3,2,1,0:T(8,128)(2,1)} fusion(bf16[2,296,16,64]{1,3,2,0:T(8,128)(2,1)S(1)} %bitcast.136, f32[2,16,296]{2,1,0:T(8,128)S(1)} %log_add_fusion, f32[2,16,296,592]{3,2,1,0:T(8,128)} %get-tuple-element.73, pred[592]{0:T(1024)(128)(4,1)S(1)} %iota_compare_fusion), kind=kOutput, calls=%fused_computation.83 | convolution fusion | flops 741392384 | bytes 26105424 | tf_op jit(solution)/shard_map/ihcs,ichd->ishd/dot_general | solution.py:173
  569.8 13.8 %fusion.113 = f32[2,16,296,592]{3,2,1,0:T(8,128)} fusion(bf16[2,296,16,64]{1,3,2,0:T(8,128)(2,1)S(1)} %bitcast.137, bf16[2,592,16,64]{1,3,2,0:T(8,128)(2,1)} %bitcast.128), kind=kOutput, calls=%fused_computation.149 | convolution fusion | flops 717750272 | bytes 26066944 | tf_op jit(solution)/shard_map/ichd,ishd->ihcs/dot_general | solution.py:170
  583.6 70.8 %fusion.59 = bf16[2,16,64,592]{3,2,1,0:T(8,128)(2,1)} fusion(bf16[2,296,16,64]{1,3,2,0:T(8,128)(2,1)} %bitcast.139, f32[2,16,296,592]{3,2,1,0:T(8,128)} %fusion.113, f32[2,16,296]{2,1,0:T(8,128)S(1)} %log_add_fusion, f32[2,16,296,592]{3,2,1,0:T(8,128)} %get-tuple-element.73, pred[592]{0:T(1024)(128)(4,1)S(1)} %iota_compare_fusion), kind=kOutput, calls=%fused_computation.82 | convolution fusion | flops 780654400 | bytes 48535120 | tf_op jit(solution)/shard_map/ihcs,ichd->ishd/dot_general | solution.py:181
  671.5 70.3 %bitcast_convert_fusion.4 = (bf16[2,296,16,64]{1,3,2,0:T(8,128)(2,1)S(1)}, f32[2,16,64,296]{3,2,1,0:T(8,128)}) fusion(bf16[2,592,16,64]{1,3,2,0:T(8,128)(2,1)} %bitcast.131, f32[2,16,296,592]{3,2,1,0:T(8,128)} %fusion.113, f32[2,16,296]{2,1,0:T(8,128)S(1)} %log_add_fusion, f32[2,16,296,592]{3,2,1,0:T(8,128)} %get-tuple-element.73, ...), kind=kOutput, calls=%fused_computation.42 | convolution fusion | flops 780048192 | bytes 50959952 | tf_op jit(solution)/shard_map/ihcs,ishd->ichd/dot_general | solution.py:178
  768.9 12.0 %bitcast_convert_fusion.1 = bf16[1024,4096]{1,0:T(8,128)(2,1)} fusion(bf16[2,296,4096]{2,1,0:T(8,128)(2,1)} %copy-done.47, f32[2,296,1024]{2,1,0:T(8,128)} %copy-done.3, f32[1024]{0:T(1024)S(1)} %bitcast.167, f32[1024]{0:T(1024)S(1)} %bitcast.158, f32[2,296]{1,0:T(2,128)S(1)} %add_rsqrt_fusion, f32[2,296]{1,0:T(2,128)S(1)} %broadcast_multiply_fusion.4), kind=kOutput, calls=%fused_computation.9 | convolution fusion | flops 4973281280 | bytes 15676032 | tf_op jit(solution)/shard_map/icd,icf->df/dot_general | solution.py:159
  781.5 42.7 %reduce-scatter.47.cloned.1.call-done = bf16[64,2]{1,0:T(8,128)(2,1)} async-done(((bf16[1024,2]{1,0:T(8,128)(2,1)}), bf16[64,2]{1,0:T(8,128)(2,1)}) %reduce-scatter.47.cloned.1.call-update) | async-done | bytes 272
  824.3 9.2 bitcast_convert_fusion.2
  833.6 49.5 %reduce-scatter.51.cloned.1.call-done = bf16[64,10]{1,0:T(8,128)(2,1)} async-done(((bf16[1024,10]{1,0:T(8,128)(2,1)}), bf16[64,10]{1,0:T(8,128)(2,1)}) %reduce-scatter.51.cloned.1.call-update) | async-done | bytes 1296
  883.2 10.7 add_convert_fusion
  894.0 95.6 %reduce-scatter.35.cloned.1.call-done = bf16[64,4096]{1,0:T(8,128)(2,1)} async-done(((bf16[1024,4096]{1,0:T(8,128)(2,1)}), bf16[64,4096]{1,0:T(8,128)(2,1)}) %reduce-scatter.35.cloned.1.call-update) | async-done | bytes 524304 | tf_op jit(solution)/shard_map/reduce_scatter | solution.py:224
  989.7 12.0 %reduce-scatter.33.cloned.1.call-done = bf16[64,512]{1,0:T(8,128)(2,1)} async-done(((bf16[64,1024]{1,0:T(8,128)(2,1)}), bf16[64,512]{1,0:T(8,128)(2,1)}) %reduce-scatter.33.cloned.1.call-update) | async-done | bytes 65552 | tf_op jit(solution)/shard_map/reduce_scatter | solution.py:241
  1014.5 88.1 %reduce-scatter.27.cloned.1.call-done = bf16[64,3072]{1,0:T(8,128)(2,1)} async-done(((bf16[1024,3072]{1,0:T(8,128)(2,1)}), bf16[64,3072]{1,0:T(8,128)(2,1)}) %reduce-scatter.27.cloned.1.call-update) | async-done | bytes 393232 | tf_op jit(solution)/shard_map/reduce_scatter | solution.py:218
  1103.2 10.3 reduce-scatter.53.cloned.1.call-done
  1115.0 15.5 %reduce-scatter.37.cloned.1.call-done = bf16[64,2048]{1,0:T(8,128)(2,1)} async-done(((bf16[64,4096]{1,0:T(8,128)(2,1)}), bf16[64,2048]{1,0:T(8,128)(2,1)}) %reduce-scatter.37.cloned.1.call-update) | async-done | bytes 262160 | tf_op jit(solution)/shard_map/reduce_scatter | solution.py:244
  1132.8 12.9 %reduce-scatter.29.cloned.1.call-done = bf16[64,1536]{1,0:T(8,128)(2,1)} async-done(((bf16[64,3072]{1,0:T(8,128)(2,1)}), bf16[64,1536]{1,0:T(8,128)(2,1)}) %reduce-scatter.29.cloned.1.call-update) | async-done | bytes 196624 | tf_op jit(solution)/shard_map/reduce_scatter | solution.py:238
  (223 shorter events, 156.5 us)
Async XLA Ops:
  7.2 73.1 %all-gather.11.cloned.1.call-start = ((), (), s32[]{:S(2)}) async-start(), calls=%async_computation.14 | async-start | bytes 6684672 | tf_op jit(solution)/shard_map/all_gather | solution.py:79
  17.1 114.9 %all-gather.13.cloned.1.call-start = ((), (), s32[]{:S(2)}) async-start(), calls=%async_computation.15 | async-start | bytes 3637248 | tf_op jit(solution)/shard_map/all_gather | solution.py:104
  69.4 219.5 %copy-start.39 = (f32[1,1024]{1,0:T(1,128)}, f32[1,1024]{1,0:T(1,128)S(1)}, u32[]{:S(2)}) copy-start(f32[1,1024]{1,0:T(1,128)S(1)} %get-tuple-element.65) | copy-start | bytes 12292
  90.7 79.6 %all-gather.15.cloned.1.call-start = ((), (), s32[]{:S(2)}) async-start(), calls=%async_computation.16 | async-start | bytes 3637248 | tf_op jit(solution)/shard_map/all_gather | solution.py:103
  93.8 120.0 %all-gather.17.cloned.1.call-start = ((), (), s32[]{:S(2)}) async-start(), calls=%async_computation.17 | async-start | bytes 2228224 | tf_op jit(solution)/shard_map/all_gather | solution.py:80
  99.0 189.9 %all-gather.19.cloned.1.call-start = ((), (), s32[]{:S(2)}) async-start(), calls=%async_computation.18 | async-start | bytes 8912896 | tf_op jit(solution)/shard_map/all_gather | solution.py:81
  114.0 300.8 %reduce-scatter.39.cloned.1.call-start = ((), (), s32[]{:S(2)}) async-start(), calls=%async_computation.26 | async-start | bytes 8912896 | tf_op jit(solution)/shard_map/reduce_scatter | solution.py:227
  114.4 186.8 %copy-start.32 = (f32[296]{0:T(512)}, f32[296]{0:T(512)S(1)}, u32[]{:S(2)}) copy-start(f32[296]{0:T(512)S(1)} %fusion.82) | copy-start | bytes 3556
  312.6 118.8 %copy-start.19 = (f32[256,512]{1,0:T(8,128)S(1)}, f32[256,512]{1,0:T(8,128)}, u32[]{:S(2)}) copy-start(f32[256,512]{1,0:T(8,128)} %param.25) | copy-start | bytes 1572868
  312.6 118.8 %copy-start.20 = (f32[256,512]{1,0:T(8,128)S(1)}, f32[256,512]{1,0:T(8,128)}, u32[]{:S(2)}) copy-start(f32[256,512]{1,0:T(8,128)} %param.31) | copy-start | bytes 1572868
  312.6 118.8 %reduce-scatter.41.cloned.1.call-start = ((), (), s32[]{:S(2)}) async-start(), calls=%async_computation.27 | async-start | bytes 786432 | tf_op jit(solution)/shard_map/reduce_scatter | solution.py:247
  414.8 102.2 %all-gather.21.cloned.1.call-start = ((), (), s32[]{:S(2)}) async-start(), calls=%async_computation.19 | async-start | bytes 8912896 | tf_op jit(solution)/shard_map/all_gather | solution.py:82
  442.6 303.0 %reduce-scatter.45.cloned.1.call-start = ((), (), s32[]{:S(2)}) async-start(), calls=%async_computation.29 | async-start | bytes 3637248
  569.5 180.8 %reduce-scatter.43.cloned.1.call-start = ((), (), s32[]{:S(2)}) async-start(), calls=%async_computation.28 | async-start | bytes 3637248
  664.8 116.2 %reduce-scatter.31.cloned.1.call-start = ((), (), s32[]{:S(2)}) async-start(), calls=%async_computation.22 | async-start | bytes 2228224 | tf_op jit(solution)/shard_map/reduce_scatter | solution.py:221
  671.1 153.1 %reduce-scatter.47.cloned.1.call-start = ((), (), s32[]{:S(2)}) async-start(), calls=%async_computation.30 | async-start | bytes 278528
  766.7 116.5 %reduce-scatter.51.cloned.1.call-start = ((), (), s32[]{:S(2)}) async-start(), calls=%async_computation.32 | async-start | bytes 278528
  768.8 220.8 %reduce-scatter.35.cloned.1.call-start = ((), (), s32[]{:S(2)}) async-start(), calls=%async_computation.24 | async-start | bytes 8912896 | tf_op jit(solution)/shard_map/reduce_scatter | solution.py:224
  780.9 220.8 %reduce-scatter.33.cloned.1.call-start = ((), (), s32[]{:S(2)}) async-start(), calls=%async_computation.23 | async-start | bytes 196608 | tf_op jit(solution)/shard_map/reduce_scatter | solution.py:241
  781.5 232.2 %reduce-scatter.49.cloned.1.call-start = ((), (), s32[]{:S(2)}) async-start(), calls=%async_computation.31 | async-start | bytes 24576
  824.2 278.3 %reduce-scatter.27.cloned.1.call-start = ((), (), s32[]{:S(2)}) async-start(), calls=%async_computation.20 | async-start | bytes 6684672 | tf_op jit(solution)/shard_map/reduce_scatter | solution.py:218
  833.6 280.0 %reduce-scatter.53.cloned.1.call-start = ((), (), s32[]{:S(2)}) async-start(), calls=%async_computation.33 | async-start | bytes 24576
  883.1 247.3 %reduce-scatter.37.cloned.1.call-start = ((), (), s32[]{:S(2)}) async-start(), calls=%async_computation.25 | async-start | bytes 786432 | tf_op jit(solution)/shard_map/reduce_scatter | solution.py:244
  883.2 118.5 %copy-start.18 = (f32[64,512]{1,0:T(8,128)S(1)}, f32[64,512]{1,0:T(8,128)}, u32[]{:S(2)}) copy-start(f32[64,512]{1,0:T(8,128)} %param.23) | copy-start | bytes 393220
  883.2 118.5 %copy-start.23 = (f32[64,512]{1,0:T(8,128)S(1)}, f32[64,512]{1,0:T(8,128)}, u32[]{:S(2)}) copy-start(f32[64,512]{1,0:T(8,128)} %param.29) | copy-start | bytes 393220
  989.6 156.1 %reduce-scatter.29.cloned.1.call-start = ((), (), s32[]{:S(2)}) async-start(), calls=%async_computation.21 | async-start | bytes 589824 | tf_op jit(solution)/shard_map/reduce_scatter | solution.py:238
  1003.4 127.0 %copy-start.8 = (f32[64,2048]{1,0:T(8,128)S(1)}, f32[64,2048]{1,0:T(8,128)}, u32[]{:S(2)}) copy-start(f32[64,2048]{1,0:T(8,128)} %param.24) | copy-start | bytes 1572868
  1003.4 127.0 %copy-start.15 = (f32[64,2048]{1,0:T(8,128)S(1)}, f32[64,2048]{1,0:T(8,128)}, u32[]{:S(2)}) copy-start(f32[64,2048]{1,0:T(8,128)} %param.30) | copy-start | bytes 1572868
  1003.4 127.0 %copy-start.16 = (f32[64,2048]{1,0:T(8,128)S(1)}, f32[64,2048]{1,0:T(8,128)}, u32[]{:S(2)}) copy-start(f32[64,2048]{1,0:T(8,128)} %param.36) | copy-start | bytes 1572868
  1007.9 137.9 %copy-start.9 = (f32[64,1536]{1,0:T(8,128)S(1)}, f32[64,1536]{1,0:T(8,128)}, u32[]{:S(2)}) copy-start(f32[64,1536]{1,0:T(8,128)} %param.22) | copy-start | bytes 1179652
  1007.9 137.9 %copy-start.21 = (f32[64,1536]{1,0:T(8,128)S(1)}, f32[64,1536]{1,0:T(8,128)}, u32[]{:S(2)}) copy-start(f32[64,1536]{1,0:T(8,128)} %param.28) | copy-start | bytes 1179652
  1007.9 137.9 %copy-start.22 = (f32[64,1536]{1,0:T(8,128)S(1)}, f32[64,1536]{1,0:T(8,128)}, u32[]{:S(2)}) copy-start(f32[64,1536]{1,0:T(8,128)} %param.34) | copy-start | bytes 1179652
  (37 other events, 1210.5 us)
Sparse Core Ops, SparseCore 0:
  17.2 63.0 all-gather.10
  90.9 41.0 all-gather.12
  133.5 36.7 all-gather.14
  172.4 41.4 all-gather.16
  215.8 73.0 all-gather.18
  312.7 102.0 reduce-scatter.38
  417.1 14.2 reduce-scatter.40
  442.7 74.2 all-gather.20
  569.7 34.1 reduce-scatter.44
  664.9 34.8 reduce-scatter.42
  703.6 61.9 reduce-scatter.30
  769.5 54.6 reduce-scatter.46
  828.3 54.7 reduce-scatter.50
  887.0 102.5 reduce-scatter.34
  991.6 9.9 reduce-scatter.32
  1003.7 9.9 reduce-scatter.48
  1017.5 85.0 reduce-scatter.26
  1104.6 8.8 reduce-scatter.52
  1115.8 14.6 reduce-scatter.36
  1132.5 13.1 reduce-scatter.28
where the time goes:
time: 1160 us; the launch traced here: 1150 us
  waiting for transfers between devices  661 us (57%)
  matrix products  294 us (25%)
  blocking collectives  86.4 us (7%)
  local copies, waits for them, and re-layouts  61.1 us (5%)
  other arithmetic  34.6 us (3%)
  between operations  15.3 us (1%)
    unnamed x26, waiting for transfers between devices  109 us
    reduce_scatter x1, waiting for transfers between devices, body(): lax.psum_scatter(g_down.astype(jnp.bfloat16), 'dp', scatter_dimension=0,...  102 us
    reduce_scatter x1, waiting for transfers between devices, body(): lax.psum_scatter(g_up.astype(jnp.bfloat16), 'dp', scatter_dimension=0, ti...  95.6 us
    reduce_scatter x1, waiting for transfers between devices, body(): lax.psum_scatter(g_qkv.astype(jnp.bfloat16), 'dp', scatter_dimension=0, t...  88.1 us
    all_gather x1, waiting for transfers between devices, body(): lax.all_gather(block_parts[3], 'dp', axis=0, tiled=True)  74.4 us
    dot_general x1, matrix products, body(): jnp.einsum('ihcs,ichd->ishd', grad_scores, query_heads, preferred_element...  70.8 us
    dot_general x1, matrix products, body(): jnp.einsum('ihcs,ishd->ichd', grad_scores, key_heads, preferred_element_t...  70.3 us
    all_gather x1, waiting for transfers between devices, body(): lax.all_gather(block_parts[2], 'dp', axis=0, tiled=True)  69.8 us
  transfers between devices with their start and end apart: 20, of which 17 were waited for; matrix products, arithmetic and copies ran while one was open for 26% of the time, Pallas kernels for 0%

commit v1 on v0

--- a/solution.py
+++ b/solution.py
@@ -6,6 +6,16 @@
 HEAD_DIM = 64
 PATCH_TOK = 577
 STEP = 5
+
+
+def ring_gather(x, axis, dim):
+    ways, here, hop = (lax.axis_size(axis), lax.axis_index(axis), x.shape[dim])
+    lengths = [n * ways if d == dim else n for d, n in enumerate(x.shape)]
+    full = lax.dynamic_update_slice_in_dim(jnp.zeros(lengths, x.dtype), x, here * hop, axis=dim)
+    for far in range(1, ways):
+        x = lax.ppermute(x, axis, [(d, (d + 1) % ways) for d in range(ways)])
+        full = lax.dynamic_update_slice_in_dim(full, x, (here - far) % ways * hop, axis=dim)
+    return full
 
 
 def normalize(rows):
@@ -78,7 +88,7 @@
     wide_qkv, wide_out, wide_up, wide_down, wide_gains, wide_biases = (
         lax.all_gather(block_parts[0], "dp", axis=0, tiled=True),
         lax.all_gather(block_parts[1], "dp", axis=0, tiled=True),
-        lax.all_gather(block_parts[2], "dp", axis=0, tiled=True),
+        ring_gather(block_parts[2], "dp", 0),
         lax.all_gather(block_parts[3], "dp", axis=0, tiled=True),
         lax.all_gather(block_parts[4], "dp", axis=1, tiled=True),
         lax.all_gather(block_parts[5], "dp", axis=1, tiled=True),

time: 1160 us -> 1200 us (1.034)
  waiting for transfers between devices: 661 us -> 685 us
  local copies, waits for them, and re-layouts: 61.1 us -> 78.7 us
    ppermute x0 -> x15, waiting for transfers between devices: none -> 149 us  [ring_gather(): x = lax.ppermute(x, axis, [(d, (d + 1) % ways) for d in range(ways)])]
    all_gather x1 -> x0, waiting for transfers between devices: 69.8 us -> none  [body(): lax.all_gather(block_parts[2], 'dp', axis=0, tiled=True)]
    all_gather x1, waiting for transfers between devices: 33.9 us -> 0.01 us  [body(): lax.all_gather(keys, 'seq', axis=1, tiled=True)]
    all_gather x1, waiting for transfers between devices: 15.7 us -> 0.02 us  [body(): lax.all_gather(values, 'seq', axis=1, tiled=True)]
    dynamic_update_slice x0 -> x16, local copies, waits for them, and re-layouts: none -> 14.4 us  [the longest x15 13.6 us: ring_gather(): lax.dynamic_update_slice_in_dim(full, x, (here - far) % ways * hop, axis=...]
    unnamed x114 -> x122, local copies, waits for them, and re-layouts: 43.1 us -> 41.6 us
    unnamed x26 -> x25, waiting for transfers between devices: 109 us -> 110 us
  transfers between devices with their start and end apart: 20 -> 34, of which waited for: 17 -> 28; matrix products, arithmetic and copies ran while one was open for 26% -> 26% of each run, Pallas kernels for 0% -> 0%
where the time goes in v1:
time: 1200 us; the launch traced here: 1190 us
  waiting for transfers between devices  685 us (57%)
  matrix products  295 us (25%)
  blocking collectives  81.7 us (7%)
  local copies, waits for them, and re-layouts  78.7 us (7%)
  other arithmetic  36 us (3%)
  between operations  15.5 us (1%)
    ppermute x15, waiting for transfers between devices, ring_gather(): x = lax.ppermute(x, axis, [(d, (d + 1) % ways) for d in range(ways)])  149 us
    unnamed x25, waiting for transfers between devices  110 us
    reduce_scatter x1, waiting for transfers between devices, body(): lax.psum_scatter(g_down.astype(jnp.bfloat16), 'dp', scatter_dimension=0,...  102 us
    reduce_scatter x1, waiting for transfers between devices, body(): lax.psum_scatter(g_up.astype(jnp.bfloat16), 'dp', scatter_dimension=0, ti...  95.8 us
    reduce_scatter x1, waiting for transfers between devices, body(): lax.psum_scatter(g_qkv.astype(jnp.bfloat16), 'dp', scatter_dimension=0, t...  88.1 us
    all_gather x1, waiting for transfers between devices, body(): lax.all_gather(block_parts[3], 'dp', axis=0, tiled=True)  74.4 us
    dot_general x1, matrix products, body(): jnp.einsum('ihcs,ichd->ishd', grad_scores, query_heads, preferred_element...  70.8 us
    dot_general x1, matrix products, body(): jnp.einsum('ihcs,ishd->ichd', grad_scores, key_heads, preferred_element_t...  70.2 us
  transfers between devices with their start and end apart: 34, of which 28 were waited for; matrix products, arithmetic and copies ran while one was open for 26% of the time, Pallas kernels for 0%

profile of v1, /device:TPU:0, one launch (start us, length us, event | category | flops | bytes accessed | tf_op | source)
XLA Modules:
  0.0 1194.2 jit_solution(18324822050004535026)
XLA Ops:
  22.2 22.7 %all-gather.3 = bf16[16,64,10]{1,2,0:T(8,128)(2,1)S(1)} all-gather(bf16[1,64,10]{1,2,0:T(8,128)(2,1)S(1)} %reshape.162), channel_id=1, replica_groups=mesh['dp'=16,'seq'=2] {'dp'}, dimensions={0}, use_global_device_ids=true | all-gather | bytes 21760 | tf_op jit(solution)/shard_map/all_gather | solution.py:94
  50.0 17.9 %all-gather.1 = bf16[16,64,2]{1,2,0:T(2,128)(2,1)S(1)} all-gather(bf16[1,64,2]{1,2,0:T(2,128)(2,1)S(1)} %reshape.158), channel_id=1, replica_groups=mesh['dp'=16,'seq'=2] {'dp'}, dimensions={0}, use_global_device_ids=true | all-gather | bytes 4352 | tf_op jit(solution)/shard_map/all_gather | solution.py:93
  90.8 9.8 all_gather.49
  100.6 11.3 collective-permute-done
  123.2 11.3 collective-permute-done.2
  135.3 10.5 collective-permute-done.3
  145.8 11.3 collective-permute-done.4
  157.9 10.6 collective-permute-done.5
  207.8 13.5 %collective-permute-done.9 = bf16[64,4096]{1,0:T(8,128)(2,1)S(1)} collective-permute-done((bf16[64,4096]{1,0:T(8,128)(2,1)S(1)}, bf16[64,4096]{1,0:T(8,128)(2,1)S(1)}, u32[]{:S(2)}, u32[]{:S(2)}) %collective-permute-start.9) | collective-permute-done | bytes 524320 | tf_op jit(solution)/shard_map/ppermute | solution.py:16
  290.2 14.1 %fusion.2 = (f32[2,16,296]{2,1,0:T(8,128)S(1)}, f32[2,16,296,592]{3,2,1,0:T(8,128)}) fusion(pred[592]{0:T(1024)(128)(4,1)S(1)} %iota_compare_fusion, bf16[2,296,16,64]{1,3,2,0:T(8,128)(2,1)S(1)} %bitcast.138, bf16[2,592,16,64]{1,3,2,0:T(8,128)(2,1)} %bitcast.130), kind=kOutput, calls=%fused_computation.7 | convolution fusion | flops 734563072 | bytes 26105424 | tf_op jit(solution)/shard_map/ichd,ishd->ihcs/dot_general | solution.py:122
  313.8 10.7 convolution_convert_fusion.1
  328.8 11.7 multiply_convert_fusion.1
  352.0 101.6 %reduce-scatter.39.cloned.1.call-done = bf16[256,1024]{1,0:T(8,128)(2,1)} async-done(((bf16[4096,1024]{1,0:T(8,128)(2,1)}), bf16[256,1024]{1,0:T(8,128)(2,1)}) %reduce-scatter.39.cloned.1.call-update) | async-done | bytes 524304 | tf_op jit(solution)/shard_map/reduce_scatter | solution.py:237
  453.7 16.3 %reduce-scatter.41.cloned.1.call-done = bf16[256,512]{1,0:T(8,128)(2,1)} async-done(((bf16[256,1024]{1,0:T(8,128)(2,1)}), bf16[256,512]{1,0:T(8,128)(2,1)}) %reduce-scatter.41.cloned.1.call-update) | async-done | bytes 262160 | tf_op jit(solution)/shard_map/reduce_scatter | solution.py:257
  481.3 74.4 %all-gather.18.cloned.1.call-done = bf16[4096,1024]{1,0:T(8,128)(2,1)} async-done(((bf16[256,1024]{1,0:T(8,128)(2,1)}), bf16[4096,1024]{1,0:T(8,128)(2,1)}) %all-gather.18.cloned.1.call-update) | async-done | bytes 8388624 | tf_op jit(solution)/shard_map/all_gather | solution.py:92
  555.7 12.6 %fusion.112 = (bf16[4096]{0:T(1024)(128)(2,1)S(1)}, bf16[2,296,4096]{2,1,0:T(8,128)(2,1)S(1)}) fusion(f32[2,296,4096]{2,1,0:T(8,128)} %get-tuple-element.77, f32[4096]{0:T(1024)S(1)} %bitcast.160, bf16[4096,1024]{1,0:T(8,128)(2,1)} %all-gather.18.cloned.1.call-done, bf16[2,296,1024]{2,1,0:T(8,128)(2,1)S(1)} %copy-done.12, f32[296]{0:T(512)} %copy-done.36), kind=kOutput, calls=%fused_computation.164 | convolution fusion | flops 4996968448 | bytes 24175776 | tf_op jit(solution)/shard_map/icd,fd->icf/dot_general | solution.py:165
  568.4 10.3 multiply_reduce_fusion.1
  585.8 12.0 %convolution_convert_fusion = bf16[2,16,64,592]{3,2,1,0:T(8,128)(2,1)} fusion(bf16[2,296,16,64]{1,3,2,0:T(8,128)(2,1)S(1)} %bitcast.136, f32[2,16,296]{2,1,0:T(8,128)S(1)} %log_add_fusion, f32[2,16,296,592]{3,2,1,0:T(8,128)} %get-tuple-element.73, pred[592]{0:T(1024)(128)(4,1)S(1)} %iota_compare_fusion), kind=kOutput, calls=%fused_computation.83 | convolution fusion | flops 741392384 | bytes 26105424 | tf_op jit(solution)/shard_map/ihcs,ichd->ishd/dot_general | solution.py:183
  608.7 13.8 %fusion.113 = f32[2,16,296,592]{3,2,1,0:T(8,128)} fusion(bf16[2,296,16,64]{1,3,2,0:T(8,128)(2,1)S(1)} %bitcast.137, bf16[2,592,16,64]{1,3,2,0:T(8,128)(2,1)} %bitcast.128), kind=kOutput, calls=%fused_computation.165 | convolution fusion | flops 717750272 | bytes 26066944 | tf_op jit(solution)/shard_map/ichd,ishd->ihcs/dot_general | solution.py:180
  622.5 70.8 %fusion.59 = bf16[2,16,64,592]{3,2,1,0:T(8,128)(2,1)} fusion(bf16[2,296,16,64]{1,3,2,0:T(8,128)(2,1)} %bitcast.139, f32[2,16,296,592]{3,2,1,0:T(8,128)} %fusion.113, f32[2,16,296]{2,1,0:T(8,128)S(1)} %log_add_fusion, f32[2,16,296,592]{3,2,1,0:T(8,128)} %get-tuple-element.73, pred[592]{0:T(1024)(128)(4,1)S(1)} %iota_compare_fusion), kind=kOutput, calls=%fused_computation.82 | convolution fusion | flops 780654400 | bytes 48535120 | tf_op jit(solution)/shard_map/ihcs,ichd->ishd/dot_general | solution.py:191
  709.0 70.2 %bitcast_convert_fusion.4 = (bf16[2,296,16,64]{1,3,2,0:T(8,128)(2,1)S(1)}, f32[2,16,64,296]{3,2,1,0:T(8,128)}) fusion(bf16[2,592,16,64]{1,3,2,0:T(8,128)(2,1)} %bitcast.131, f32[2,16,296,592]{3,2,1,0:T(8,128)} %fusion.113, f32[2,16,296]{2,1,0:T(8,128)S(1)} %log_add_fusion, f32[2,16,296,592]{3,2,1,0:T(8,128)} %get-tuple-element.73, ...), kind=kOutput, calls=%fused_computation.42 | convolution fusion | flops 780048192 | bytes 50959952 | tf_op jit(solution)/shard_map/ihcs,ishd->ichd/dot_general | solution.py:188
  793.8 9.8 fusion.46
  806.8 12.0 %bitcast_convert_fusion.1 = bf16[1024,4096]{1,0:T(8,128)(2,1)} fusion(bf16[2,296,4096]{2,1,0:T(8,128)(2,1)} %copy-done.51, f32[2,296,1024]{2,1,0:T(8,128)} %copy-done.3, f32[1024]{0:T(1024)S(1)} %bitcast.167, f32[1024]{0:T(1024)S(1)} %bitcast.158, f32[2,296]{1,0:T(2,128)S(1)} %add_rsqrt_fusion, f32[2,296]{1,0:T(2,128)S(1)} %broadcast_multiply_fusion.4), kind=kOutput, calls=%fused_computation.9 | convolution fusion | flops 4973281280 | bytes 15676032 | tf_op jit(solution)/shard_map/icd,icf->df/dot_general | solution.py:169
  819.4 44.0 %reduce-scatter.47.cloned.1.call-done = bf16[64,2]{1,0:T(8,128)(2,1)} async-done(((bf16[1024,2]{1,0:T(8,128)(2,1)}), bf16[64,2]{1,0:T(8,128)(2,1)}) %reduce-scatter.47.cloned.1.call-update) | async-done | bytes 272
  872.8 49.3 %reduce-scatter.51.cloned.1.call-done = bf16[64,10]{1,0:T(8,128)(2,1)} async-done(((bf16[1024,10]{1,0:T(8,128)(2,1)}), bf16[64,10]{1,0:T(8,128)(2,1)}) %reduce-scatter.51.cloned.1.call-update) | async-done | bytes 1296
  922.3 10.7 add_convert_fusion
  933.0 95.8 %reduce-scatter.35.cloned.1.call-done = bf16[64,4096]{1,0:T(8,128)(2,1)} async-done(((bf16[1024,4096]{1,0:T(8,128)(2,1)}), bf16[64,4096]{1,0:T(8,128)(2,1)}) %reduce-scatter.35.cloned.1.call-update) | async-done | bytes 524304 | tf_op jit(solution)/shard_map/reduce_scatter | solution.py:234
  1028.9 12.0 %reduce-scatter.33.cloned.1.call-done = bf16[64,512]{1,0:T(8,128)(2,1)} async-done(((bf16[64,1024]{1,0:T(8,128)(2,1)}), bf16[64,512]{1,0:T(8,128)(2,1)}) %reduce-scatter.33.cloned.1.call-update) | async-done | bytes 65552 | tf_op jit(solution)/shard_map/reduce_scatter | solution.py:251
  1053.7 88.1 %reduce-scatter.27.cloned.1.call-done = bf16[64,3072]{1,0:T(8,128)(2,1)} async-done(((bf16[1024,3072]{1,0:T(8,128)(2,1)}), bf16[64,3072]{1,0:T(8,128)(2,1)}) %reduce-scatter.27.cloned.1.call-update) | async-done | bytes 393232 | tf_op jit(solution)/shard_map/reduce_scatter | solution.py:228
  1142.5 10.5 reduce-scatter.53.cloned.1.call-done
  1154.4 15.3 %reduce-scatter.37.cloned.1.call-done = bf16[64,2048]{1,0:T(8,128)(2,1)} async-done(((bf16[64,4096]{1,0:T(8,128)(2,1)}), bf16[64,2048]{1,0:T(8,128)(2,1)}) %reduce-scatter.37.cloned.1.call-update) | async-done | bytes 262160 | tf_op jit(solution)/shard_map/reduce_scatter | solution.py:254
  1172.1 13.1 %reduce-scatter.29.cloned.1.call-done = bf16[64,1536]{1,0:T(8,128)(2,1)} async-done(((bf16[64,3072]{1,0:T(8,128)(2,1)}), bf16[64,1536]{1,0:T(8,128)(2,1)}) %reduce-scatter.29.cloned.1.call-update) | async-done | bytes 196624 | tf_op jit(solution)/shard_map/reduce_scatter | solution.py:248
  (275 shorter events, 280.6 us)
Async XLA Ops:
  7.2 73.1 %all-gather.10.cloned.1.call-start = ((), (), s32[]{:S(2)}) async-start(), calls=%async_computation.14 | async-start | bytes 6684672 | tf_op jit(solution)/shard_map/all_gather | solution.py:89
  17.1 264.0 %all-gather.12.cloned.1.call-start = ((), (), s32[]{:S(2)}) async-start(), calls=%async_computation.15 | async-start | bytes 3637248 | tf_op jit(solution)/shard_map/all_gather | solution.py:114
  90.7 195.2 %all-gather.14.cloned.1.call-start = ((), (), s32[]{:S(2)}) async-start(), calls=%async_computation.16 | async-start | bytes 3637248 | tf_op jit(solution)/shard_map/all_gather | solution.py:113
  100.6 11.3 collective-permute-start
  111.9 11.3 collective-permute-start.1
  114.8 209.7 %all-gather.16.cloned.1.call-start = ((), (), s32[]{:S(2)}) async-start(), calls=%async_computation.17 | async-start | bytes 2228224 | tf_op jit(solution)/shard_map/all_gather | solution.py:90
  123.2 11.3 collective-permute-start.2
  134.5 11.3 collective-permute-start.3
  145.8 11.3 collective-permute-start.4
  157.1 11.4 collective-permute-start.5
  168.5 11.5 collective-permute-start.6
  174.1 279.5 %reduce-scatter.39.cloned.1.call-start = ((), (), s32[]{:S(2)}) async-start(), calls=%async_computation.25 | async-start | bytes 8912896 | tf_op jit(solution)/shard_map/reduce_scatter | solution.py:237
  180.0 14.6 %collective-permute-start.7 = (bf16[64,4096]{1,0:T(8,128)(2,1)S(1)}, bf16[64,4096]{1,0:T(8,128)(2,1)S(1)}, u32[]{:S(2)}, u32[]{:S(2)}) collective-permute-start(bf16[64,4096]{1,0:T(8,128)(2,1)S(1)} %collective-permute-done.6), channel_id=1, source_target_pairs={{0,2},{2,4},{4,6},{6,8},{8,10},{10,12},{12,14},{14,16},{16,18},{18... | collective-permute-start | bytes 1572872 | tf_op jit(solution)/shard_map/ppermute | solution.py:16
  194.7 11.5 collective-permute-start.8
  206.1 15.2 %collective-permute-start.9 = (bf16[64,4096]{1,0:T(8,128)(2,1)S(1)}, bf16[64,4096]{1,0:T(8,128)(2,1)S(1)}, u32[]{:S(2)}, u32[]{:S(2)}) collective-permute-start(bf16[64,4096]{1,0:T(8,128)(2,1)S(1)} %collective-permute-done.8), channel_id=1, source_target_pairs={{0,2},{2,4},{4,6},{6,8},{8,10},{10,12},{12,14},{14,16},{16,18},{18... | collective-permute-start | bytes 1572872 | tf_op jit(solution)/shard_map/ppermute | solution.py:16
  232.6 11.3 collective-permute-start.11
  243.9 11.3 collective-permute-start.12
  266.5 11.8 collective-permute-start.14
  352.0 118.0 %reduce-scatter.41.cloned.1.call-start = ((), (), s32[]{:S(2)}) async-start(), calls=%async_computation.26 | async-start | bytes 786432 | tf_op jit(solution)/shard_map/reduce_scatter | solution.py:257
  453.6 102.1 %all-gather.18.cloned.1.call-start = ((), (), s32[]{:S(2)}) async-start(), calls=%async_computation.18 | async-start | bytes 8912896 | tf_op jit(solution)/shard_map/all_gather | solution.py:92
  481.3 301.8 %reduce-scatter.45.cloned.1.call-start = ((), (), s32[]{:S(2)}) async-start(), calls=%async_computation.28 | async-start | bytes 3637248
  608.2 179.6 %reduce-scatter.43.cloned.1.call-start = ((), (), s32[]{:S(2)}) async-start(), calls=%async_computation.27 | async-start | bytes 3637248
  703.9 115.0 %reduce-scatter.31.cloned.1.call-start = ((), (), s32[]{:S(2)}) async-start(), calls=%async_computation.21 | async-start | bytes 2228224 | tf_op jit(solution)/shard_map/reduce_scatter | solution.py:231
  708.8 154.6 %reduce-scatter.47.cloned.1.call-start = ((), (), s32[]{:S(2)}) async-start(), calls=%async_computation.29 | async-start | bytes 278528
  804.5 117.7 %reduce-scatter.51.cloned.1.call-start = ((), (), s32[]{:S(2)}) async-start(), calls=%async_computation.31 | async-start | bytes 278528
  806.7 222.1 %reduce-scatter.35.cloned.1.call-start = ((), (), s32[]{:S(2)}) async-start(), calls=%async_computation.23 | async-start | bytes 8912896 | tf_op jit(solution)/shard_map/reduce_scatter | solution.py:234
  818.8 222.1 %reduce-scatter.33.cloned.1.call-start = ((), (), s32[]{:S(2)}) async-start(), calls=%async_computation.22 | async-start | bytes 196608 | tf_op jit(solution)/shard_map/reduce_scatter | solution.py:251
  819.4 233.6 %reduce-scatter.49.cloned.1.call-start = ((), (), s32[]{:S(2)}) async-start(), calls=%async_computation.30 | async-start | bytes 24576
  863.5 278.4 %reduce-scatter.27.cloned.1.call-start = ((), (), s32[]{:S(2)}) async-start(), calls=%async_computation.19 | async-start | bytes 6684672 | tf_op jit(solution)/shard_map/reduce_scatter | solution.py:228
  872.8 280.2 %reduce-scatter.53.cloned.1.call-start = ((), (), s32[]{:S(2)}) async-start(), calls=%async_computation.32 | async-start | bytes 24576
  922.2 247.5 %reduce-scatter.37.cloned.1.call-start = ((), (), s32[]{:S(2)}) async-start(), calls=%async_computation.24 | async-start | bytes 786432 | tf_op jit(solution)/shard_map/reduce_scatter | solution.py:254
  1028.9 156.3 %reduce-scatter.29.cloned.1.call-start = ((), (), s32[]{:S(2)}) async-start(), calls=%async_computation.20 | async-start | bytes 589824 | tf_op jit(solution)/shard_map/reduce_scatter | solution.py:248
  (55 other events, 2808.3 us)
Sparse Core Ops, SparseCore 0:
  17.2 63.0 all-gather.9
  90.8 35.4 all-gather.11
  127.9 37.4 all-gather.13
  174.2 46.5 all-gather.15
  352.1 101.4 reduce-scatter.38
  455.7 14.2 reduce-scatter.40
  481.4 74.2 all-gather.17
  608.4 34.0 reduce-scatter.44
  704.0 34.8 reduce-scatter.42
  742.4 62.1 reduce-scatter.30
  808.7 54.6 reduce-scatter.46
  867.4 54.7 reduce-scatter.50
  926.2 102.5 reduce-scatter.34
  1030.9 9.9 reduce-scatter.32
  1043.0 9.9 reduce-scatter.48
  1056.7 85.0 reduce-scatter.26
  1143.9 9.0 reduce-scatter.52
  1155.1 14.6 reduce-scatter.36
  1172.0 13.1 reduce-scatter.28
